TPU v7x, 32 devices: a whole 2x2x4 slice. The times are simulated.
32 devices in a mesh: gx: 4 (over y, core), gy: 8 (over z, x).
Axes of the slice: x: 2, y: 2, z: 4, core: 2. Of those that a mesh axis runs over, the one named last changes fastest.
Arguments:
- source: float32 [256, 128, 128], P('gx', 'gy'), may hold values from -6 to 6
- diagonal: float32 [256, 128, 128], P('gx', 'gy'), may hold values from 6.05 to 7
- face_x: float32 [256, 128, 128], P('gx', 'gy'), may hold values from 0.1 to 1
- face_y: float32 [256, 128, 128], P('gx', 'gy'), may hold values from 0.1 to 1
- face_z: float32 [256, 128, 128], P('gx', 'gy'), may hold values from 0.1 to 1
- iterates: float32 [8, 256, 128, 128], P(None, 'gx', 'gy'), may hold values from -0.3 to 0.3
- labels: int32 [256, 128], P('gx', 'gy'), may hold values from 0 to 7
Outputs:
- new_iterates: float32 [8, 256, 128, 128], P(None, 'gx', 'gy')
- new_residual: float32 [256, 128, 128], P('gx', 'gy')
All inputs are finite; a program needn't handle non-finite values.
Results may differ from a plain program's by a relative error of at most 0.0003.
Values sent between devices are 32-bit elements; how exact they have to be, the bound alone decides.
No kernel may reach another device: no remote copies, remote signals or barrier semaphores. Data moves between devices by JAX's collectives and lax.ppermute only.
A program may use at most 128 MiB of HBM per device.

v0:
```python
import jax
import jax.numpy as jnp
from jax import lax
from jax.sharding import PartitionSpec as P

ENLARGE = 8
basis_shift = 6.5


def padded_2(block, sides, width):
    for axis, dim in sides:
        count = lax.axis_size(axis)
        forward = [(i, i + 1) for i in range(count - 1)]
        backward = [(target, source) for source, target in forward]
        low = lax.ppermute(
            lax.slice_in_dim(block, block.shape[dim] - width, None, axis=dim), axis, forward
        )
        high = lax.ppermute(lax.slice_in_dim(block, 0, width, axis=dim), axis, backward)
        block = jnp.concatenate([low, block, high], axis=dim)
    return block


def stencil(values, face_x, face_y, face_z, diagonal):
    centre = values[..., 1:-1, 1:-1, :]
    result = diagonal * centre
    result = (
        result
        - face_x[1:-1, 1:-1, :] * values[..., 2:, 1:-1, :]
        - face_x[:-2, 1:-1, :] * values[..., :-2, 1:-1, :]
    )
    result = (
        result
        - face_y[1:-1, 1:-1, :] * values[..., 1:-1, 2:, :]
        - face_y[1:-1, :-2, :] * values[..., 1:-1, :-2, :]
    )
    widths = [(0, 0)] * (centre.ndim - 1) + [(1, 1)]
    padded = jnp.pad(centre, widths)
    lower_face = jnp.pad(face_z[..., :-1], ((0, 0), (0, 0), (1, 0)))
    return result - face_z * padded[..., 2:] - lower_face * padded[..., :-2]


def finish(gram, project):
    highest = lax.Precision.HIGHEST
    lower = jnp.linalg.cholesky(gram)
    ident = jnp.eye(gram.shape[0], dtype=gram.dtype)
    inverse = lax.linalg.triangular_solve(lower, ident, left_side=True, lower=True)
    reduced = jnp.dot(jnp.dot(inverse, project, precision=highest), inverse.T, precision=highest)
    reduced = 0.5 * (reduced + reduced.T)
    target = jnp.dot(inverse, gram[:, :ENLARGE], precision=highest)
    factor = jnp.linalg.cholesky(reduced)
    middle = lax.linalg.triangular_solve(factor, target, left_side=True, lower=True)
    solved = lax.linalg.triangular_solve(
        factor, middle, left_side=True, lower=True, transpose_a=True
    )
    return jnp.dot(inverse.T, solved, precision=highest)


def shards(source, diagonal, face_x, face_y, face_z, iterates, labels):
    highest = lax.Precision.HIGHEST
    summed = jnp.sum(iterates, axis=0)
    columns = jnp.arange(ENLARGE, dtype=jnp.int32)
    near = (
        padded_2(summed, (("gx", 0), ("gy", 1)), 1),
        padded_2(face_x, (("gx", 0), ("gy", 1)), 1),
        padded_2(face_y, (("gx", 0), ("gy", 1)), 1),
    )
    near_sum, near_fx, near_fy = near
    residual = source - stencil(near_sum, near_fx, near_fy, face_z, diagonal)
    onehot = (labels[None] == columns[:, None, None]).astype(jnp.float32)
    blocks = residual[None] * onehot[..., None]
    blocks_wide = padded_2(blocks, (("gx", 1), ("gy", 2)), 1)
    applied = stencil(blocks_wide, near_fx, near_fy, face_z, diagonal)
    powered = applied - basis_shift * blocks
    powered_wide = padded_2(powered, (("gx", 1), ("gy", 2)), 1)
    second = stencil(powered_wide, near_fx, near_fy, face_z, diagonal)
    basis = jnp.concatenate([blocks, powered], axis=0)
    image = jnp.concatenate([applied, second], axis=0)
    gram_local = jnp.einsum("aijk,bijk->ab", basis, basis, precision=highest)
    project_local = jnp.einsum("aijk,bijk->ab", basis, image, precision=highest)
    gram = lax.psum(gram_local, ("gx", "gy"))
    project = lax.psum(project_local, ("gx", "gy"))
    coeffs = finish(gram, project)
    new_iterates = iterates + jnp.einsum("ab,aijk->bijk", coeffs, basis, precision=highest)
    carried = jnp.sum(coeffs, axis=1)
    new_residual = residual - jnp.einsum("a,aijk->ijk", carried, image, precision=highest)
    return (new_iterates, new_residual)


def solution(mesh):
    placed = (
        P("gx", "gy", None),
        P("gx", "gy", None),
        P("gx", "gy", None),
        P("gx", "gy", None),
        P("gx", "gy", None),
        P(None, "gx", "gy", None),
        P("gx", "gy"),
    )
    return jax.shard_map(
        shards,
        mesh=mesh,
        in_specs=placed,
        out_specs=(P(None, "gx", "gy", None), P("gx", "gy", None)),
        check_vma=False,
    )
```

profile of v0, /device:TPU:0, one launch (start us, length us, event | category | flops | bytes accessed | tf_op | source)
XLA Modules:
  0.0 177.3 jit_solution(15040397435094770270)
XLA Ops:
  0.7 2.7 %reduce_sum.18 = f32[64,16,128]{2,1,0:T(8,128)S(1)} reduce(f32[8,64,16,128]{3,2,1,0:T(8,128)} %param.13, f32[]{:T(128)} %constant.43.clone.1), dimensions={0}, to_apply=%region_0.0 | reduce | flops 917504 | bytes 4718596 | tf_op jit(solution)/shard_map/reduce_sum | solution.py:60
  3.4 1.3 collective-permute-start
  4.7 3.0 %collective-permute-start.2 = (f32[1,16,128]{2,1,0:T(8,128)S(1)}, f32[1,16,128]{2,1,0:T(8,128)S(1)}, u32[]{:S(2)}, u32[]{:S(2)}) collective-permute-start(f32[1,16,128]{2,1,0:T(8,128)S(1)} %get-tuple-element.23), channel_id=1, source_target_pairs={{0,8},{8,16},{16,24},{1,9},{9,17},{17,25},{2,10},{10,18},{18,26},{... | collective-permute-start | bytes 24584 | tf_op jit(solution)/shard_map/ppermute | solution.py:15
  7.7 4.5 %collective-permute-start.4 = (f32[1,16,128]{2,1,0:T(8,128)S(1)}, f32[1,16,128]{2,1,0:T(8,128)S(1)}, u32[]{:S(2)}, u32[]{:S(2)}) collective-permute-start(f32[1,16,128]{2,1,0:T(8,128)S(1)} %get-tuple-element.22), channel_id=1, source_target_pairs={{0,8},{8,16},{16,24},{1,9},{9,17},{17,25},{2,10},{10,18},{18,26},{... | collective-permute-start | bytes 24584 | tf_op jit(solution)/shard_map/ppermute | solution.py:15
  12.2 1.3 collective-permute-start.5
  13.6 3.0 %collective-permute-start.1 = (f32[1,16,128]{2,1,0:T(8,128)S(1)}, f32[1,16,128]{2,1,0:T(8,128)S(1)}, u32[]{:S(2)}, u32[]{:S(2)}) collective-permute-start(f32[1,16,128]{2,1,0:T(8,128)S(1)} %slice.156), channel_id=1, source_target_pairs={{0,8},{8,16},{16,24},{1,9},{9,17},{17,25},{2,10},{10,18},{18,26},{... | collective-permute-start | bytes 24584 | tf_op jit(solution)/shard_map/ppermute | solution.py:15
  16.8 1.3 collective-permute-start.3
  18.1 4.5 %collective-permute-start.7 = (f32[66,1,128]{2,1,0:T(1,128)S(1)}, f32[66,1,128]{2,1,0:T(1,128)S(1)}, u32[]{:S(2)}, u32[]{:S(2)}) collective-permute-start(f32[66,1,128]{2,1,0:T(1,128)S(1)} %get-tuple-element.20), channel_id=1, source_target_pairs={{0,1},{1,2},{2,3},{3,4},{4,5},{5,6},{6,7},{8,9},{9,10},{10,11},{11... | collective-permute-start | bytes 101384 | tf_op jit(solution)/shard_map/ppermute | solution.py:15
  22.7 4.3 %collective-permute-start.6 = (f32[66,1,128]{2,1,0:T(1,128)S(1)}, f32[66,1,128]{2,1,0:T(1,128)S(1)}, u32[]{:S(2)}, u32[]{:S(2)}) collective-permute-start(f32[66,1,128]{2,1,0:T(1,128)S(1)} %slice.194), channel_id=1, source_target_pairs={{0,1},{1,2},{2,3},{3,4},{4,5},{5,6},{6,7},{8,9},{9,10},{10,11},{11... | collective-permute-start | bytes 101384 | tf_op jit(solution)/shard_map/ppermute | solution.py:15
  27.3 1.3 collective-permute-done.6
  28.6 1.6 fusion.33
  31.5 1.3 collective-permute-start.8
  32.8 3.0 %collective-permute-start.9 = (f32[8,1,16,128]{3,0,2,1:T(8,128)S(1)}, f32[8,1,16,128]{3,0,2,1:T(8,128)S(1)}, u32[]{:S(2)}, u32[]{:S(2)}) collective-permute-start(f32[8,1,16,128]{3,0,2,1:T(8,128)S(1)} %get-tuple-element.17), channel_id=1, source_target_pairs={{0,8},{8,16},{16,24},{1,9},{9,17},{17,25},{2,10},{10,18},{18,26},{... | collective-permute-start | bytes 196616 | tf_op jit(solution)/shard_map/ppermute | solution.py:15
  36.8 1.3 collective-permute-start.10
  38.1 5.0 %collective-permute-start.11 = (f32[8,66,1,128]{3,0,2,1:T(8,128)S(1)}, f32[8,66,1,128]{3,0,2,1:T(8,128)S(1)}, u32[]{:S(2)}, u32[]{:S(2)}) collective-permute-start(f32[8,66,1,128]{3,0,2,1:T(8,128)S(1)} %get-tuple-element.14), channel_id=1, source_target_pairs={{0,1},{1,2},{2,3},{3,4},{4,5},{5,6},{6,7},{8,9},{9,10},{10,11},{11... | collective-permute-start | bytes 811016 | tf_op jit(solution)/shard_map/ppermute | solution.py:15
  43.4 4.0 %collective-permute-done.10 = f32[8,66,1,128]{3,0,2,1:T(8,128)S(1)} collective-permute-done((f32[8,66,1,128]{3,0,2,1:T(8,128)S(1)}, f32[8,66,1,128]{3,0,2,1:T(8,128)S(1)}, u32[]{:S(2)}, u32[]{:S(2)}) %collective-permute-start.10) | collective-permute-done | bytes 270368 | tf_op jit(solution)/shard_map/ppermute | solution.py:18
  47.4 7.2 %collective-permute-done.11 = f32[8,66,1,128]{3,0,2,1:T(8,128)S(1)} collective-permute-done((f32[8,66,1,128]{3,0,2,1:T(8,128)S(1)}, f32[8,66,1,128]{3,0,2,1:T(8,128)S(1)}, u32[]{:S(2)}, u32[]{:S(2)}) %collective-permute-start.11) | collective-permute-done | bytes 270368 | tf_op jit(solution)/shard_map/ppermute | solution.py:15
  54.6 7.5 %multiply_subtract_fusion = (f32[8,64,16,128]{3,0,2,1:T(8,128)S(1)}, f32[8,64,16,128]{3,0,2,1:T(8,128)S(1)}) fusion(f32[8,64,16]{0,2,1:T(8,128)S(1)} %fusion.43, f32[64,16,128]{2,1,0:T(8,128)S(1)} %get-tuple-element.9, f32[64,16,128]{2,1,0:T(8,128)S(1)} %pad.18, f32[8,64,16,128]{3,0,2,1:T(8,128)S(1)} %broadcast_multiply_fusion, ...), kind=kLoop, calls=%fused_computation.51 | loop fusion | flops 25165824 | bytes 17481728 | tf_op jit(solution)/shard_map/sub | solution.py:73
  62.1 1.3 collective-permute-start.12
  63.4 3.0 %collective-permute-start.13 = (f32[8,1,16,128]{3,0,2,1:T(8,128)S(1)}, f32[8,1,16,128]{3,0,2,1:T(8,128)S(1)}, u32[]{:S(2)}, u32[]{:S(2)}) collective-permute-start(f32[8,1,16,128]{3,0,2,1:T(8,128)S(1)} %get-tuple-element.15), channel_id=1, source_target_pairs={{0,8},{8,16},{16,24},{1,9},{9,17},{17,25},{2,10},{10,18},{18,26},{... | collective-permute-start | bytes 196616 | tf_op jit(solution)/shard_map/ppermute | solution.py:15
  67.4 1.3 collective-permute-start.14
  68.7 5.0 %collective-permute-start.15 = (f32[8,66,1,128]{3,0,2,1:T(8,128)S(1)}, f32[8,66,1,128]{3,0,2,1:T(8,128)S(1)}, u32[]{:S(2)}, u32[]{:S(2)}) collective-permute-start(f32[8,66,1,128]{3,0,2,1:T(8,128)S(1)} %get-tuple-element.12), channel_id=1, source_target_pairs={{0,1},{1,2},{2,3},{3,4},{4,5},{5,6},{6,7},{8,9},{9,10},{10,11},{11... | collective-permute-start | bytes 811016 | tf_op jit(solution)/shard_map/ppermute | solution.py:15
  73.7 11.2 %fusion.28 = f32[16,16]{0,1:T(8,128)S(1)} fusion(f32[8,64,16,128]{3,0,2,1:T(8,128)S(1)} %get-tuple-element.7, f32[8,64,16,128]{3,0,2,1:T(8,128)S(1)} %broadcast_multiply_fusion), kind=kOutput, calls=%fused_computation.55 | convolution fusion | flops 404750336 | bytes 8389632 | tf_op jit(solution)/shard_map/aijk,bijk->ab/dot_general | solution.py:78
  85.3 6.8 %fusion.10 = f32[8,64,16,128]{3,0,2,1:T(8,128)S(1)} fusion(f32[8,64,16,128]{3,0,2,1:T(8,128)S(1)} %get-tuple-element.7, f32[8,66,1,128]{3,0,2,1:T(8,128)S(1)} %collective-permute-done.15, f32[8,1,16,128]{3,0,2,1:T(8,128)S(1)} %collective-permute-done.12, f32[8,1,16,128]{3,0,2,1:T(8,128)S(1)} %collective-permute-done.13, ...), kind=kLoop, calls=%fused_computation.16 | loop fusion | flops 22020096 | bytes 12730368 | tf_op jit(solution)/shard_map/sub | solution.py:39
  92.1 1.9 %copy-done.5 = f32[8,64,16,128]{3,0,2,1:T(8,128)} copy-done((f32[8,64,16,128]{3,0,2,1:T(8,128)}, f32[8,64,16,128]{3,0,2,1:T(8,128)S(1)}, u32[]{:S(2)}) %copy-start.5) | copy-done | bytes 4194328
  94.1 10.4 %fusion.29 = f32[16,16]{1,0:T(8,128)S(1)} fusion(f32[8,64,16,128]{3,0,2,1:T(8,128)S(1)} %fusion.10, f32[8,64,16,128]{3,0,2,1:T(8,128)S(1)} %get-tuple-element.8, f32[8,64,16,128]{3,0,2,1:T(8,128)S(1)} %get-tuple-element.7, f32[8,64,16,128]{3,0,2,1:T(8,128)S(1)} %broadcast_multiply_fusion), kind=kOutput, calls=%fused_computation.56 | convolution fusion | flops 406847488 | bytes 16778240 | tf_op jit(solution)/shard_map/aijk,bijk->ab/dot_general | solution.py:79
  104.5 44.6 %all-reduce.4 = (f32[16,16]{0,1:T(8,128)S(1)}, f32[16,16]{1,0:T(8,128)S(1)}) all-reduce(f32[16,16]{0,1:T(8,128)S(1)} %fusion.28, f32[16,16]{1,0:T(8,128)S(1)} %fusion.29), channel_id=1, replica_groups=mesh['gx'=4,'gy'=8] {'gx','gy'}, use_global_device_ids=true, to_apply=%region_1.2 | all-reduce | flops 512 | bytes 4096 | tf_op jit(solution)/shard_map/psum | solution.py:80
  149.1 1.5 cholesky.44
  153.9 1.5 cholesky.55
  158.5 6.6 %fusion = f32[1,64,16,128]{3,0,2,1:T(1,128)S(1)} fusion(f32[8,64,16,128]{3,0,2,1:T(8,128)} %copy-done.5, f32[8,64,16,128]{3,0,2,1:T(8,128)} %copy-done.4, f32[16]{0:T(128)S(1)} %get-tuple-element.25), kind=kOutput, calls=%fused_computation.6 | convolution fusion | flops 27262976 | bytes 8912960 | tf_op jit(solution)/shard_map/a,aijk->ijk/dot_general | solution.py:85
  166.0 8.6 %copy_add_fusion = f32[8,64,16,128]{3,0,2,1:T(8,128)S(1)} fusion(f32[8,64,16,128]{3,2,1,0:T(8,128)} %param.13, f32[8,64,16,128]{3,0,2,1:T(8,128)S(1)} %copy-done.3, f32[8,64,16,128]{3,0,2,1:T(8,128)S(1)} %copy-done.1, f32[16,8]{0,1:T(8,128)S(1)} %get-tuple-element.26), kind=kOutput, calls=%fused_computation.50 | convolution fusion | flops 204472320 | bytes 16777728 | tf_op jit(solution)/shard_map/ab,aijk->bijk/dot_general | solution.py:83
  174.6 2.8 %copy.15 = f32[8,64,16,128]{3,2,1,0:T(8,128)} copy(f32[8,64,16,128]{3,0,2,1:T(8,128)S(1)} %copy_add_fusion) | data formatting | bytes 8388608
  (73 shorter events, 11.6 us)
Async XLA Ops:
  0.6 7.1 %copy-start.7 = (f32[64,16,128]{2,1,0:T(8,128)S(1)}, f32[64,16,128]{2,1,0:T(8,128)}, u32[]{:S(2)}) copy-start(f32[64,16,128]{2,1,0:T(8,128)} %param.11) | copy-start | bytes 1572868
  0.6 12.9 %copy-start.8 = (f32[64,16,128]{2,1,0:T(8,128)S(1)}, f32[64,16,128]{2,1,0:T(8,128)}, u32[]{:S(2)}) copy-start(f32[64,16,128]{2,1,0:T(8,128)} %param.10) | copy-start | bytes 1572868
  0.7 15.9 %copy-start.10 = (s32[64,16]{0,1:T(8,128)S(1)}, s32[64,16]{0,1:T(8,128)}, u32[]{:S(2)}) copy-start(s32[64,16]{0,1:T(8,128)} %param.14) | copy-start | bytes 12292
  0.7 28.0 %copy-start.6 = (f32[64,16,128]{2,1,0:T(8,128)S(1)}, f32[64,16,128]{2,1,0:T(8,128)}, u32[]{:S(2)}) copy-start(f32[64,16,128]{2,1,0:T(8,128)} %param.12) | copy-start | bytes 1572868
  0.7 28.0 %copy-start.9 = (f32[64,16,128]{2,1,0:T(8,128)S(1)}, f32[64,16,128]{2,1,0:T(8,128)}, u32[]{:S(2)}) copy-start(f32[64,16,128]{2,1,0:T(8,128)} %param.9) | copy-start | bytes 1572868
  3.4 13.3 %collective-permute-start = (f32[1,16,128]{2,1,0:T(8,128)S(1)}, f32[1,16,128]{2,1,0:T(8,128)S(1)}, u32[]{:S(2)}, u32[]{:S(2)}) collective-permute-start(f32[1,16,128]{2,1,0:T(8,128)S(1)} %get-tuple-element.24), channel_id=1, source_target_pairs={{8,0},{16,8},{24,16},{9,1},{17,9},{25,17},{10,2},{18,10},{26,18},{... | collective-permute-start | bytes 24584 | tf_op jit(solution)/shard_map/ppermute | solution.py:18
  4.7 12.0 %collective-permute-start.2 = (f32[1,16,128]{2,1,0:T(8,128)S(1)}, f32[1,16,128]{2,1,0:T(8,128)S(1)}, u32[]{:S(2)}, u32[]{:S(2)}) collective-permute-start(f32[1,16,128]{2,1,0:T(8,128)S(1)} %get-tuple-element.23), channel_id=1, source_target_pairs={{0,8},{8,16},{16,24},{1,9},{9,17},{17,25},{2,10},{10,18},{18,26},{... | collective-permute-start | bytes 24584 | tf_op jit(solution)/shard_map/ppermute | solution.py:15
  7.7 14.9 %collective-permute-start.4 = (f32[1,16,128]{2,1,0:T(8,128)S(1)}, f32[1,16,128]{2,1,0:T(8,128)S(1)}, u32[]{:S(2)}, u32[]{:S(2)}) collective-permute-start(f32[1,16,128]{2,1,0:T(8,128)S(1)} %get-tuple-element.22), channel_id=1, source_target_pairs={{0,8},{8,16},{16,24},{1,9},{9,17},{17,25},{2,10},{10,18},{18,26},{... | collective-permute-start | bytes 24584 | tf_op jit(solution)/shard_map/ppermute | solution.py:15
  12.2 10.4 %collective-permute-start.5 = (f32[1,16,128]{2,1,0:T(8,128)S(1)}, f32[1,16,128]{2,1,0:T(8,128)S(1)}, u32[]{:S(2)}, u32[]{:S(2)}) collective-permute-start(f32[1,16,128]{2,1,0:T(8,128)S(1)} %get-tuple-element.21), channel_id=1, source_target_pairs={{8,0},{16,8},{24,16},{9,1},{17,9},{25,17},{10,2},{18,10},{26,18},{... | collective-permute-start | bytes 24584 | tf_op jit(solution)/shard_map/ppermute | solution.py:18
  13.6 13.7 %collective-permute-start.1 = (f32[1,16,128]{2,1,0:T(8,128)S(1)}, f32[1,16,128]{2,1,0:T(8,128)S(1)}, u32[]{:S(2)}, u32[]{:S(2)}) collective-permute-start(f32[1,16,128]{2,1,0:T(8,128)S(1)} %slice.156), channel_id=1, source_target_pairs={{0,8},{8,16},{16,24},{1,9},{9,17},{17,25},{2,10},{10,18},{18,26},{... | collective-permute-start | bytes 24584 | tf_op jit(solution)/shard_map/ppermute | solution.py:15
  16.8 10.5 %collective-permute-start.3 = (f32[66,1,128]{2,1,0:T(1,128)S(1)}, f32[66,1,128]{2,1,0:T(1,128)S(1)}, u32[]{:S(2)}, u32[]{:S(2)}) collective-permute-start(f32[66,1,128]{2,1,0:T(1,128)S(1)} %get-tuple-element.19), channel_id=1, source_target_pairs={{1,0},{2,1},{3,2},{4,3},{5,4},{6,5},{7,6},{9,8},{10,9},{11,10},{12... | collective-permute-start | bytes 101384 | tf_op jit(solution)/shard_map/ppermute | solution.py:18
  18.1 9.2 %collective-permute-start.7 = (f32[66,1,128]{2,1,0:T(1,128)S(1)}, f32[66,1,128]{2,1,0:T(1,128)S(1)}, u32[]{:S(2)}, u32[]{:S(2)}) collective-permute-start(f32[66,1,128]{2,1,0:T(1,128)S(1)} %get-tuple-element.20), channel_id=1, source_target_pairs={{0,1},{1,2},{2,3},{3,4},{4,5},{5,6},{6,7},{8,9},{9,10},{10,11},{11... | collective-permute-start | bytes 101384 | tf_op jit(solution)/shard_map/ppermute | solution.py:15
  22.7 5.9 %collective-permute-start.6 = (f32[66,1,128]{2,1,0:T(1,128)S(1)}, f32[66,1,128]{2,1,0:T(1,128)S(1)}, u32[]{:S(2)}, u32[]{:S(2)}) collective-permute-start(f32[66,1,128]{2,1,0:T(1,128)S(1)} %slice.194), channel_id=1, source_target_pairs={{0,1},{1,2},{2,3},{3,4},{4,5},{5,6},{6,7},{8,9},{9,10},{10,11},{11... | collective-permute-start | bytes 101384 | tf_op jit(solution)/shard_map/ppermute | solution.py:15
  31.5 60.6 %copy-start = (f32[8,64,16,128]{3,0,2,1:T(8,128)}, f32[8,64,16,128]{3,0,2,1:T(8,128)S(1)}, u32[]{:S(2)}) copy-start(f32[8,64,16,128]{3,0,2,1:T(8,128)S(1)} %broadcast_multiply_fusion) | copy-start | bytes 12582916
  31.5 4.3 %collective-permute-start.8 = (f32[8,1,16,128]{3,0,2,1:T(8,128)S(1)}, f32[8,1,16,128]{3,0,2,1:T(8,128)S(1)}, u32[]{:S(2)}, u32[]{:S(2)}) collective-permute-start(f32[8,1,16,128]{3,0,2,1:T(8,128)S(1)} %get-tuple-element.18), channel_id=1, source_target_pairs={{8,0},{16,8},{24,16},{9,1},{17,9},{25,17},{10,2},{18,10},{26,18},{... | collective-permute-start | bytes 196616 | tf_op jit(solution)/shard_map/ppermute | solution.py:18
  32.8 3.9 %collective-permute-start.9 = (f32[8,1,16,128]{3,0,2,1:T(8,128)S(1)}, f32[8,1,16,128]{3,0,2,1:T(8,128)S(1)}, u32[]{:S(2)}, u32[]{:S(2)}) collective-permute-start(f32[8,1,16,128]{3,0,2,1:T(8,128)S(1)} %get-tuple-element.17), channel_id=1, source_target_pairs={{0,8},{8,16},{16,24},{1,9},{9,17},{17,25},{2,10},{10,18},{18,26},{... | collective-permute-start | bytes 196616 | tf_op jit(solution)/shard_map/ppermute | solution.py:15
  36.8 10.6 %collective-permute-start.10 = (f32[8,66,1,128]{3,0,2,1:T(8,128)S(1)}, f32[8,66,1,128]{3,0,2,1:T(8,128)S(1)}, u32[]{:S(2)}, u32[]{:S(2)}) collective-permute-start(f32[8,66,1,128]{3,0,2,1:T(8,128)S(1)} %get-tuple-element.13), channel_id=1, source_target_pairs={{1,0},{2,1},{3,2},{4,3},{5,4},{6,5},{7,6},{9,8},{10,9},{11,10},{12... | collective-permute-start | bytes 811016 | tf_op jit(solution)/shard_map/ppermute | solution.py:18
  38.1 16.6 %collective-permute-start.11 = (f32[8,66,1,128]{3,0,2,1:T(8,128)S(1)}, f32[8,66,1,128]{3,0,2,1:T(8,128)S(1)}, u32[]{:S(2)}, u32[]{:S(2)}) collective-permute-start(f32[8,66,1,128]{3,0,2,1:T(8,128)S(1)} %get-tuple-element.14), channel_id=1, source_target_pairs={{0,1},{1,2},{2,3},{3,4},{4,5},{5,6},{6,7},{8,9},{9,10},{10,11},{11... | collective-permute-start | bytes 811016 | tf_op jit(solution)/shard_map/ppermute | solution.py:15
  62.1 30.0 %copy-start.2 = (f32[8,64,16,128]{3,0,2,1:T(8,128)}, f32[8,64,16,128]{3,0,2,1:T(8,128)S(1)}, u32[]{:S(2)}) copy-start(f32[8,64,16,128]{3,0,2,1:T(8,128)S(1)} %get-tuple-element.7) | copy-start | bytes 12582916
  62.1 30.0 %copy-start.4 = (f32[8,64,16,128]{3,0,2,1:T(8,128)}, f32[8,64,16,128]{3,0,2,1:T(8,128)S(1)}, u32[]{:S(2)}) copy-start(f32[8,64,16,128]{3,0,2,1:T(8,128)S(1)} %get-tuple-element.8) | copy-start | bytes 12582916
  62.1 4.3 %collective-permute-start.12 = (f32[8,1,16,128]{3,0,2,1:T(8,128)S(1)}, f32[8,1,16,128]{3,0,2,1:T(8,128)S(1)}, u32[]{:S(2)}, u32[]{:S(2)}) collective-permute-start(f32[8,1,16,128]{3,0,2,1:T(8,128)S(1)} %get-tuple-element.16), channel_id=1, source_target_pairs={{8,0},{16,8},{24,16},{9,1},{17,9},{25,17},{10,2},{18,10},{26,18},{... | collective-permute-start | bytes 196616 | tf_op jit(solution)/shard_map/ppermute | solution.py:18
  63.4 3.9 %collective-permute-start.13 = (f32[8,1,16,128]{3,0,2,1:T(8,128)S(1)}, f32[8,1,16,128]{3,0,2,1:T(8,128)S(1)}, u32[]{:S(2)}, u32[]{:S(2)}) collective-permute-start(f32[8,1,16,128]{3,0,2,1:T(8,128)S(1)} %get-tuple-element.15), channel_id=1, source_target_pairs={{0,8},{8,16},{16,24},{1,9},{9,17},{17,25},{2,10},{10,18},{18,26},{... | collective-permute-start | bytes 196616 | tf_op jit(solution)/shard_map/ppermute | solution.py:15
  67.4 17.5 %collective-permute-start.14 = (f32[8,66,1,128]{3,0,2,1:T(8,128)S(1)}, f32[8,66,1,128]{3,0,2,1:T(8,128)S(1)}, u32[]{:S(2)}, u32[]{:S(2)}) collective-permute-start(f32[8,66,1,128]{3,0,2,1:T(8,128)S(1)} %get-tuple-element.11), channel_id=1, source_target_pairs={{1,0},{2,1},{3,2},{4,3},{5,4},{6,5},{7,6},{9,8},{10,9},{11,10},{12... | collective-permute-start | bytes 811016 | tf_op jit(solution)/shard_map/ppermute | solution.py:18
  68.7 16.6 %collective-permute-start.15 = (f32[8,66,1,128]{3,0,2,1:T(8,128)S(1)}, f32[8,66,1,128]{3,0,2,1:T(8,128)S(1)}, u32[]{:S(2)}, u32[]{:S(2)}) collective-permute-start(f32[8,66,1,128]{3,0,2,1:T(8,128)S(1)} %get-tuple-element.12), channel_id=1, source_target_pairs={{0,1},{1,2},{2,3},{3,4},{4,5},{5,6},{6,7},{8,9},{9,10},{10,11},{11... | collective-permute-start | bytes 811016 | tf_op jit(solution)/shard_map/ppermute | solution.py:15
  92.1 2.0 %copy-start.5 = (f32[8,64,16,128]{3,0,2,1:T(8,128)}, f32[8,64,16,128]{3,0,2,1:T(8,128)S(1)}, u32[]{:S(2)}) copy-start(f32[8,64,16,128]{3,0,2,1:T(8,128)S(1)} %fusion.10) | copy-start | bytes 12582916
  158.5 7.5 %copy-start.1 = (f32[8,64,16,128]{3,0,2,1:T(8,128)S(1)}, f32[8,64,16,128]{3,0,2,1:T(8,128)}, u32[]{:S(2)}) copy-start(f32[8,64,16,128]{3,0,2,1:T(8,128)} %copy-done) | copy-start | bytes 12582916
  158.5 7.5 %copy-start.3 = (f32[8,64,16,128]{3,0,2,1:T(8,128)S(1)}, f32[8,64,16,128]{3,0,2,1:T(8,128)}, u32[]{:S(2)}) copy-start(f32[8,64,16,128]{3,0,2,1:T(8,128)} %copy-done.2) | copy-start | bytes 12582916
where the time goes:
time: 178 us; the launch traced here: 177 us
  starting transfers between devices  44.6 us (25%)
  blocking collectives  44.6 us (25%)
  matrix products  37.9 us (21%)
  other arithmetic  29 us (16%)
  waiting for transfers between devices  14.8 us (8%)
  local copies, waits for them, and re-layouts  5.36 us (3%)
    psum x1, blocking collectives, shards(): gram = lax.psum(gram_local, ('gx', 'gy'))  44.6 us
    ppermute x9, starting transfers between devices, padded_2(): lax.ppermute(lax.slice_in_dim(block, block.shape[dim] - width, None, axis...  35.5 us
    dot_general x1, matrix products, shards(): gram_local = jnp.einsum('aijk,bijk->ab', basis, basis, precision=highest)  11.2 us
    ppermute x9, waiting for transfers between devices, padded_2(): lax.ppermute(lax.slice_in_dim(block, block.shape[dim] - width, None, axis...  10.7 us
    dot_general x1, matrix products, shards(): project_local = jnp.einsum('aijk,bijk->ab', basis, image, precision=highest)  10.4 us
    ppermute x7, starting transfers between devices, padded_2(): lax.ppermute(lax.slice_in_dim(block, 0, width, axis=dim), axis, backward)  9.04 us
    dot_general x1, matrix products, shards(): jnp.einsum('ab,aijk->bijk', coeffs, basis, precision=highest)  8.56 us
    sub x1, other arithmetic, shards(): powered = applied - basis_shift * blocks  7.45 us
  transfers between devices with their start and end apart: 16, of which 6 were waited for; matrix products, arithmetic and copies ran while one was open for 7% of the time, Pallas kernels for 0%

commit v1 on v0

--- a/solution.py
+++ b/solution.py
@@ -77,7 +77,8 @@
     image = jnp.concatenate([applied, second], axis=0)
     gram_local = jnp.einsum("aijk,bijk->ab", basis, basis, precision=highest)
     project_local = jnp.einsum("aijk,bijk->ab", basis, image, precision=highest)
-    gram = lax.psum(gram_local, ("gx", "gy"))
+    x_now = lax.all_gather(gram_local, ("gx", "gy"))
+    gram = jnp.sum(x_now, 0)
     project = lax.psum(project_local, ("gx", "gy"))
     coeffs = finish(gram, project)
     new_iterates = iterates + jnp.einsum("ab,aijk->bijk", coeffs, basis, precision=highest)

time: 178 us -> 248 us (1.39)
  blocking collectives: 44.6 us -> 108 us
  other arithmetic: 29 us -> 32.3 us
    all_gather x0 -> x1, blocking collectives: none -> 67.5 us  [shards(): x_now = lax.all_gather(gram_local, ('gx', 'gy'))]
    psum x1, blocking collectives: 44.6 us -> 40.4 us  [shards(): project = lax.psum(project_local, ('gx', 'gy'))]
  transfers between devices with their start and end apart: 16 -> 16, of which waited for: 6 -> 6; matrix products, arithmetic and copies ran while one was open for 7% -> 2% of each run, Pallas kernels for 0% -> 0%
where the time goes in v1:
time: 248 us; the launch traced here: 247 us
  blocking collectives  108 us (44%)
  starting transfers between devices  44.4 us (18%)
  matrix products  38.1 us (15%)
  other arithmetic  32.3 us (13%)
  waiting for transfers between devices  17.1 us (7%)
  local copies, waits for them, and re-layouts  6.09 us (2%)
    all_gather x1, blocking collectives, shards(): x_now = lax.all_gather(gram_local, ('gx', 'gy'))  67.5 us
    psum x1, blocking collectives, shards(): project = lax.psum(project_local, ('gx', 'gy'))  40.4 us
    ppermute x9, starting transfers between devices, padded_2(): lax.ppermute(lax.slice_in_dim(block, block.shape[dim] - width, None, axis...  35.1 us
    dot_general x1, matrix products, shards(): gram_local = jnp.einsum('aijk,bijk->ab', basis, basis, precision=highest)  11.4 us
    ppermute x9, waiting for transfers between devices, padded_2(): lax.ppermute(lax.slice_in_dim(block, block.shape[dim] - width, None, axis...  10.9 us
    dot_general x1, matrix products, shards(): project_local = jnp.einsum('aijk,bijk->ab', basis, image, precision=highest)  10.4 us
    ppermute x7, starting transfers between devices, padded_2(): lax.ppermute(lax.slice_in_dim(block, 0, width, axis=dim), axis, backward)  9.32 us
    dot_general x1, matrix products, shards(): jnp.einsum('ab,aijk->bijk', coeffs, basis, precision=highest)  8.56 us
  transfers between devices with their start and end apart: 16, of which 6 were waited for; matrix products, arithmetic and copies ran while one was open for 2% of the time, Pallas kernels for 0%

profile of v1, /device:TPU:0, one launch (start us, length us, event | category | flops | bytes accessed | tf_op | source)
XLA Modules:
  0.0 247.0 jit_solution(3787354743446300611)
XLA Ops:
  0.7 2.7 %reduce_sum.27 = f32[64,16,128]{2,1,0:T(8,128)S(1)} reduce(f32[8,64,16,128]{3,2,1,0:T(8,128)} %param.13, f32[]{:T(128)} %constant.43.clone.1), dimensions={0}, to_apply=%region_0.0 | reduce | flops 917504 | bytes 4718596 | tf_op jit(solution)/shard_map/reduce_sum | solution.py:60
  3.4 1.3 collective-permute-start
  4.7 3.0 %collective-permute-start.2 = (f32[1,16,128]{2,1,0:T(8,128)S(1)}, f32[1,16,128]{2,1,0:T(8,128)S(1)}, u32[]{:S(2)}, u32[]{:S(2)}) collective-permute-start(f32[1,16,128]{2,1,0:T(8,128)S(1)} %get-tuple-element.23), channel_id=1, source_target_pairs={{0,8},{8,16},{16,24},{1,9},{9,17},{17,25},{2,10},{10,18},{18,26},{... | collective-permute-start | bytes 24584 | tf_op jit(solution)/shard_map/ppermute | solution.py:15
  7.7 4.5 %collective-permute-start.4 = (f32[1,16,128]{2,1,0:T(8,128)S(1)}, f32[1,16,128]{2,1,0:T(8,128)S(1)}, u32[]{:S(2)}, u32[]{:S(2)}) collective-permute-start(f32[1,16,128]{2,1,0:T(8,128)S(1)} %get-tuple-element.22), channel_id=1, source_target_pairs={{0,8},{8,16},{16,24},{1,9},{9,17},{17,25},{2,10},{10,18},{18,26},{... | collective-permute-start | bytes 24584 | tf_op jit(solution)/shard_map/ppermute | solution.py:15
  13.6 3.0 %collective-permute-start.1 = (f32[1,16,128]{2,1,0:T(8,128)S(1)}, f32[1,16,128]{2,1,0:T(8,128)S(1)}, u32[]{:S(2)}, u32[]{:S(2)}) collective-permute-start(f32[1,16,128]{2,1,0:T(8,128)S(1)} %slice.156), channel_id=1, source_target_pairs={{0,8},{8,16},{16,24},{1,9},{9,17},{17,25},{2,10},{10,18},{18,26},{... | collective-permute-start | bytes 24584 | tf_op jit(solution)/shard_map/ppermute | solution.py:15
  18.1 4.5 %collective-permute-start.7 = (f32[66,1,128]{2,1,0:T(1,128)S(1)}, f32[66,1,128]{2,1,0:T(1,128)S(1)}, u32[]{:S(2)}, u32[]{:S(2)}) collective-permute-start(f32[66,1,128]{2,1,0:T(1,128)S(1)} %get-tuple-element.20), channel_id=1, source_target_pairs={{0,1},{1,2},{2,3},{3,4},{4,5},{5,6},{6,7},{8,9},{9,10},{10,11},{11... | collective-permute-start | bytes 101384 | tf_op jit(solution)/shard_map/ppermute | solution.py:15
  22.7 4.3 %collective-permute-start.6 = (f32[66,1,128]{2,1,0:T(1,128)S(1)}, f32[66,1,128]{2,1,0:T(1,128)S(1)}, u32[]{:S(2)}, u32[]{:S(2)}) collective-permute-start(f32[66,1,128]{2,1,0:T(1,128)S(1)} %slice.194), channel_id=1, source_target_pairs={{0,1},{1,2},{2,3},{3,4},{4,5},{5,6},{6,7},{8,9},{9,10},{10,11},{11... | collective-permute-start | bytes 101384 | tf_op jit(solution)/shard_map/ppermute | solution.py:15
  27.3 1.3 collective-permute-done.6
  28.6 1.6 fusion.33
  31.5 1.4 collective-permute-start.8
  33.0 3.0 %collective-permute-start.9 = (f32[8,1,16,128]{3,0,2,1:T(8,128)S(1)}, f32[8,1,16,128]{3,0,2,1:T(8,128)S(1)}, u32[]{:S(2)}, u32[]{:S(2)}) collective-permute-start(f32[8,1,16,128]{3,0,2,1:T(8,128)S(1)} %get-tuple-element.17), channel_id=1, source_target_pairs={{0,8},{8,16},{16,24},{1,9},{9,17},{17,25},{2,10},{10,18},{18,26},{... | collective-permute-start | bytes 196616 | tf_op jit(solution)/shard_map/ppermute | solution.py:15
  38.2 5.0 %collective-permute-start.11 = (f32[8,66,1,128]{3,0,2,1:T(8,128)S(1)}, f32[8,66,1,128]{3,0,2,1:T(8,128)S(1)}, u32[]{:S(2)}, u32[]{:S(2)}) collective-permute-start(f32[8,66,1,128]{3,0,2,1:T(8,128)S(1)} %get-tuple-element.14), channel_id=1, source_target_pairs={{0,1},{1,2},{2,3},{3,4},{4,5},{5,6},{6,7},{8,9},{9,10},{10,11},{11... | collective-permute-start | bytes 811016 | tf_op jit(solution)/shard_map/ppermute | solution.py:15
  43.5 4.0 %collective-permute-done.10 = f32[8,66,1,128]{3,0,2,1:T(8,128)S(1)} collective-permute-done((f32[8,66,1,128]{3,0,2,1:T(8,128)S(1)}, f32[8,66,1,128]{3,0,2,1:T(8,128)S(1)}, u32[]{:S(2)}, u32[]{:S(2)}) %collective-permute-start.10) | collective-permute-done | bytes 270368 | tf_op jit(solution)/shard_map/ppermute | solution.py:18
  47.6 7.2 %collective-permute-done.11 = f32[8,66,1,128]{3,0,2,1:T(8,128)S(1)} collective-permute-done((f32[8,66,1,128]{3,0,2,1:T(8,128)S(1)}, f32[8,66,1,128]{3,0,2,1:T(8,128)S(1)}, u32[]{:S(2)}, u32[]{:S(2)}) %collective-permute-start.11) | collective-permute-done | bytes 270368 | tf_op jit(solution)/shard_map/ppermute | solution.py:15
  54.8 8.3 %multiply_subtract_fusion = (f32[8,64,16,128]{3,0,2,1:T(8,128)S(1)}, f32[8,64,16,128]{3,0,2,1:T(8,128)}) fusion(f32[8,64,16]{0,2,1:T(8,128)S(1)} %fusion.43, f32[64,16,128]{2,1,0:T(8,128)S(1)} %get-tuple-element.9, f32[64,16,128]{2,1,0:T(8,128)S(1)} %pad.18, f32[8,64,16,128]{3,0,2,1:T(8,128)S(1)} %broadcast_multiply_fusion, f32[64,16,128]{2,1,0:T(8,128)S(1)} %copy-done.8, ...), kind=kLoop, calls=%fused_computation.51 | loop fusion | flops 25165824 | bytes 17481728 | tf_op jit(solution)/shard_map/sub | solution.py:73
  63.8 11.4 %fusion.28 = f32[16,16]{1,0:T(8,128)S(1)} fusion(f32[8,64,16,128]{3,0,2,1:T(8,128)S(1)} %get-tuple-element.7, f32[8,64,16,128]{3,0,2,1:T(8,128)S(1)} %broadcast_multiply_fusion), kind=kOutput, calls=%fused_computation.55 | convolution fusion | flops 404750336 | bytes 8389632 | tf_op jit(solution)/shard_map/aijk,bijk->ab/dot_general | solution.py:78
  75.2 1.3 collective-permute-start.12
  76.5 3.0 %collective-permute-start.13 = (f32[8,1,16,128]{3,0,2,1:T(8,128)}, f32[8,1,16,128]{3,0,2,1:T(8,128)S(1)}, u32[]{:S(2)}, u32[]{:S(2)}) collective-permute-start(f32[8,1,16,128]{3,0,2,1:T(8,128)} %get-tuple-element.15), channel_id=1, source_target_pairs={{0,8},{8,16},{16,24},{1,9},{9,17},{17,25},{2,10},{10,18},{18,26},{... | collective-permute-start | bytes 196616 | tf_op jit(solution)/shard_map/ppermute | solution.py:15
  79.6 67.5 %all-gather = f32[512,16]{1,0:T(8,128)S(1)} all-gather(f32[16,16]{1,0:T(8,128)S(1)} %fusion.28), channel_id=2, replica_groups=mesh['gx'=4,'gy'=8] {'gx','gy'}, dimensions={0}, use_global_device_ids=true | all-gather | bytes 33792 | tf_op jit(solution)/shard_map/all_gather | solution.py:80
  147.2 1.5 cholesky.44
  152.6 1.4 collective-permute-start.14
  154.0 4.6 %collective-permute-start.15 = (f32[8,66,1,128]{3,0,2,1:T(8,128)S(1)}, f32[8,66,1,128]{3,0,2,1:T(8,128)S(1)}, u32[]{:S(2)}, u32[]{:S(2)}) collective-permute-start(f32[8,66,1,128]{3,0,2,1:T(8,128)S(1)} %get-tuple-element.12), channel_id=1, source_target_pairs={{0,1},{1,2},{2,3},{3,4},{4,5},{5,6},{6,7},{8,9},{9,10},{10,11},{11... | collective-permute-start | bytes 811016 | tf_op jit(solution)/shard_map/ppermute | solution.py:15
  159.0 2.1 collective-permute-done.14
  161.1 1.5 collective-permute-done.15
  162.6 7.9 %fusion.10 = f32[8,64,16,128]{3,0,2,1:T(8,128)S(1)} fusion(f32[8,64,16,128]{3,0,2,1:T(8,128)S(1)} %copy-done.4, f32[8,66,1,128]{3,0,2,1:T(8,128)S(1)} %collective-permute-done.15, f32[8,1,16,128]{3,0,2,1:T(8,128)S(1)} %collective-permute-done.12, f32[8,1,16,128]{3,0,2,1:T(8,128)S(1)} %collective-permute-done.13, ...), kind=kLoop, calls=%fused_computation.16 | loop fusion | flops 22020096 | bytes 12730368 | tf_op jit(solution)/shard_map/sub | solution.py:39
  170.4 2.0 copy-done.7
  172.4 10.4 %fusion.29 = f32[16,16]{1,0:T(8,128)S(1)} fusion(f32[8,64,16,128]{3,0,2,1:T(8,128)S(1)} %fusion.10, f32[8,64,16,128]{3,0,2,1:T(8,128)S(1)} %copy-done.6, f32[8,64,16,128]{3,0,2,1:T(8,128)S(1)} %copy-done.4, f32[8,64,16,128]{3,0,2,1:T(8,128)S(1)} %copy-done.1), kind=kOutput, calls=%fused_computation.56 | convolution fusion | flops 406847488 | bytes 16778240 | tf_op jit(solution)/shard_map/aijk,bijk->ab/dot_general | solution.py:79
  182.8 40.4 %psum.7 = f32[16,16]{1,0:T(8,128)S(1)} all-reduce(f32[16,16]{1,0:T(8,128)S(1)} %fusion.29), channel_id=1, replica_groups=mesh['gx'=4,'gy'=8] {'gx','gy'}, use_global_device_ids=true, to_apply=%region_4.6 | all-reduce | flops 256 | bytes 2048 | tf_op jit(solution)/shard_map/psum | solution.py:82
  223.6 1.5 cholesky.55
  228.2 6.6 %fusion = f32[1,64,16,128]{3,0,2,1:T(1,128)S(1)} fusion(f32[8,64,16,128]{3,0,2,1:T(8,128)} %copy-done.7, f32[8,64,16,128]{3,0,2,1:T(8,128)} %get-tuple-element.8, f32[16]{0:T(128)S(1)} %get-tuple-element.25), kind=kOutput, calls=%fused_computation.6 | convolution fusion | flops 27262976 | bytes 8912960 | tf_op jit(solution)/shard_map/a,aijk->ijk/dot_general | solution.py:86
  235.7 8.6 %copy_add_fusion = f32[8,64,16,128]{3,0,2,1:T(8,128)S(1)} fusion(f32[8,64,16,128]{3,2,1,0:T(8,128)} %param.13, f32[8,64,16,128]{3,0,2,1:T(8,128)S(1)} %copy-done.5, f32[8,64,16,128]{3,0,2,1:T(8,128)S(1)} %copy-done.2, f32[16,8]{0,1:T(8,128)S(1)} %get-tuple-element.26), kind=kOutput, calls=%fused_computation.50 | convolution fusion | flops 204472320 | bytes 16777728 | tf_op jit(solution)/shard_map/ab,aijk->bijk/dot_general | solution.py:84
  244.2 2.8 %copy.20 = f32[8,64,16,128]{3,2,1,0:T(8,128)} copy(f32[8,64,16,128]{3,0,2,1:T(8,128)S(1)} %copy_add_fusion) | data formatting | bytes 8388608
  (85 shorter events, 16.2 us)
Async XLA Ops:
  0.6 7.1 %copy-start.9 = (f32[64,16,128]{2,1,0:T(8,128)S(1)}, f32[64,16,128]{2,1,0:T(8,128)}, u32[]{:S(2)}) copy-start(f32[64,16,128]{2,1,0:T(8,128)} %param.11) | copy-start | bytes 1572868
  0.6 12.9 %copy-start.10 = (f32[64,16,128]{2,1,0:T(8,128)S(1)}, f32[64,16,128]{2,1,0:T(8,128)}, u32[]{:S(2)}) copy-start(f32[64,16,128]{2,1,0:T(8,128)} %param.10) | copy-start | bytes 1572868
  0.7 16.0 %copy-start.15 = (s32[64,16]{0,1:T(8,128)S(1)}, s32[64,16]{0,1:T(8,128)}, u32[]{:S(2)}) copy-start(s32[64,16]{0,1:T(8,128)} %param.14) | copy-start | bytes 12292
  0.7 28.0 %copy-start.8 = (f32[64,16,128]{2,1,0:T(8,128)S(1)}, f32[64,16,128]{2,1,0:T(8,128)}, u32[]{:S(2)}) copy-start(f32[64,16,128]{2,1,0:T(8,128)} %param.12) | copy-start | bytes 1572868
  0.7 28.0 %copy-start.11 = (f32[64,16,128]{2,1,0:T(8,128)S(1)}, f32[64,16,128]{2,1,0:T(8,128)}, u32[]{:S(2)}) copy-start(f32[64,16,128]{2,1,0:T(8,128)} %param.9) | copy-start | bytes 1572868
  3.4 13.3 %collective-permute-start = (f32[1,16,128]{2,1,0:T(8,128)S(1)}, f32[1,16,128]{2,1,0:T(8,128)S(1)}, u32[]{:S(2)}, u32[]{:S(2)}) collective-permute-start(f32[1,16,128]{2,1,0:T(8,128)S(1)} %get-tuple-element.24), channel_id=1, source_target_pairs={{8,0},{16,8},{24,16},{9,1},{17,9},{25,17},{10,2},{18,10},{26,18},{... | collective-permute-start | bytes 24584 | tf_op jit(solution)/shard_map/ppermute | solution.py:18
  4.7 12.0 %collective-permute-start.2 = (f32[1,16,128]{2,1,0:T(8,128)S(1)}, f32[1,16,128]{2,1,0:T(8,128)S(1)}, u32[]{:S(2)}, u32[]{:S(2)}) collective-permute-start(f32[1,16,128]{2,1,0:T(8,128)S(1)} %get-tuple-element.23), channel_id=1, source_target_pairs={{0,8},{8,16},{16,24},{1,9},{9,17},{17,25},{2,10},{10,18},{18,26},{... | collective-permute-start | bytes 24584 | tf_op jit(solution)/shard_map/ppermute | solution.py:15
  7.7 14.9 %collective-permute-start.4 = (f32[1,16,128]{2,1,0:T(8,128)S(1)}, f32[1,16,128]{2,1,0:T(8,128)S(1)}, u32[]{:S(2)}, u32[]{:S(2)}) collective-permute-start(f32[1,16,128]{2,1,0:T(8,128)S(1)} %get-tuple-element.22), channel_id=1, source_target_pairs={{0,8},{8,16},{16,24},{1,9},{9,17},{17,25},{2,10},{10,18},{18,26},{... | collective-permute-start | bytes 24584 | tf_op jit(solution)/shard_map/ppermute | solution.py:15
  12.2 10.4 %collective-permute-start.5 = (f32[1,16,128]{2,1,0:T(8,128)S(1)}, f32[1,16,128]{2,1,0:T(8,128)S(1)}, u32[]{:S(2)}, u32[]{:S(2)}) collective-permute-start(f32[1,16,128]{2,1,0:T(8,128)S(1)} %get-tuple-element.21), channel_id=1, source_target_pairs={{8,0},{16,8},{24,16},{9,1},{17,9},{25,17},{10,2},{18,10},{26,18},{... | collective-permute-start | bytes 24584 | tf_op jit(solution)/shard_map/ppermute | solution.py:18
  13.6 13.7 %collective-permute-start.1 = (f32[1,16,128]{2,1,0:T(8,128)S(1)}, f32[1,16,128]{2,1,0:T(8,128)S(1)}, u32[]{:S(2)}, u32[]{:S(2)}) collective-permute-start(f32[1,16,128]{2,1,0:T(8,128)S(1)} %slice.156), channel_id=1, source_target_pairs={{0,8},{8,16},{16,24},{1,9},{9,17},{17,25},{2,10},{10,18},{18,26},{... | collective-permute-start | bytes 24584 | tf_op jit(solution)/shard_map/ppermute | solution.py:15
  16.8 10.5 %collective-permute-start.3 = (f32[66,1,128]{2,1,0:T(1,128)S(1)}, f32[66,1,128]{2,1,0:T(1,128)S(1)}, u32[]{:S(2)}, u32[]{:S(2)}) collective-permute-start(f32[66,1,128]{2,1,0:T(1,128)S(1)} %get-tuple-element.19), channel_id=1, source_target_pairs={{1,0},{2,1},{3,2},{4,3},{5,4},{6,5},{7,6},{9,8},{10,9},{11,10},{12... | collective-permute-start | bytes 101384 | tf_op jit(solution)/shard_map/ppermute | solution.py:18
  18.1 9.2 %collective-permute-start.7 = (f32[66,1,128]{2,1,0:T(1,128)S(1)}, f32[66,1,128]{2,1,0:T(1,128)S(1)}, u32[]{:S(2)}, u32[]{:S(2)}) collective-permute-start(f32[66,1,128]{2,1,0:T(1,128)S(1)} %get-tuple-element.20), channel_id=1, source_target_pairs={{0,1},{1,2},{2,3},{3,4},{4,5},{5,6},{6,7},{8,9},{9,10},{10,11},{11... | collective-permute-start | bytes 101384 | tf_op jit(solution)/shard_map/ppermute | solution.py:15
  22.7 5.9 %collective-permute-start.6 = (f32[66,1,128]{2,1,0:T(1,128)S(1)}, f32[66,1,128]{2,1,0:T(1,128)S(1)}, u32[]{:S(2)}, u32[]{:S(2)}) collective-permute-start(f32[66,1,128]{2,1,0:T(1,128)S(1)} %slice.194), channel_id=1, source_target_pairs={{0,1},{1,2},{2,3},{3,4},{4,5},{5,6},{6,7},{8,9},{9,10},{10,11},{11... | collective-permute-start | bytes 101384 | tf_op jit(solution)/shard_map/ppermute | solution.py:15
  30.2 24.6 %copy-start.14 = (f32[64,16,128]{2,1,0:T(8,128)}, f32[64,16,128]{2,1,0:T(8,128)S(1)}, u32[]{:S(2)}) copy-start(f32[64,16,128]{2,1,0:T(8,128)S(1)} %get-tuple-element.10) | copy-start | bytes 1572868
  31.5 32.3 %copy-start = (f32[8,64,16,128]{3,0,2,1:T(8,128)}, f32[8,64,16,128]{3,0,2,1:T(8,128)S(1)}, u32[]{:S(2)}) copy-start(f32[8,64,16,128]{3,0,2,1:T(8,128)S(1)} %broadcast_multiply_fusion) | copy-start | bytes 12582916
  31.5 23.3 %copy-start.12 = (f32[64,16,128]{2,1,0:T(8,128)S(1)}, f32[64,16,128]{2,1,0:T(8,128)}, u32[]{:S(2)}) copy-start(f32[64,16,128]{2,1,0:T(8,128)} %param.9) | copy-start | bytes 1572868
  31.5 4.5 %collective-permute-start.8 = (f32[8,1,16,128]{3,0,2,1:T(8,128)S(1)}, f32[8,1,16,128]{3,0,2,1:T(8,128)S(1)}, u32[]{:S(2)}, u32[]{:S(2)}) collective-permute-start(f32[8,1,16,128]{3,0,2,1:T(8,128)S(1)} %get-tuple-element.18), channel_id=1, source_target_pairs={{8,0},{16,8},{24,16},{9,1},{17,9},{25,17},{10,2},{18,10},{26,18},{... | collective-permute-start | bytes 196616 | tf_op jit(solution)/shard_map/ppermute | solution.py:18
  33.0 3.9 %collective-permute-start.9 = (f32[8,1,16,128]{3,0,2,1:T(8,128)S(1)}, f32[8,1,16,128]{3,0,2,1:T(8,128)S(1)}, u32[]{:S(2)}, u32[]{:S(2)}) collective-permute-start(f32[8,1,16,128]{3,0,2,1:T(8,128)S(1)} %get-tuple-element.17), channel_id=1, source_target_pairs={{0,8},{8,16},{16,24},{1,9},{9,17},{17,25},{2,10},{10,18},{18,26},{... | collective-permute-start | bytes 196616 | tf_op jit(solution)/shard_map/ppermute | solution.py:15
  36.9 10.6 %collective-permute-start.10 = (f32[8,66,1,128]{3,0,2,1:T(8,128)S(1)}, f32[8,66,1,128]{3,0,2,1:T(8,128)S(1)}, u32[]{:S(2)}, u32[]{:S(2)}) collective-permute-start(f32[8,66,1,128]{3,0,2,1:T(8,128)S(1)} %get-tuple-element.13), channel_id=1, source_target_pairs={{1,0},{2,1},{3,2},{4,3},{5,4},{6,5},{7,6},{9,8},{10,9},{11,10},{12... | collective-permute-start | bytes 811016 | tf_op jit(solution)/shard_map/ppermute | solution.py:18
  38.2 16.6 %collective-permute-start.11 = (f32[8,66,1,128]{3,0,2,1:T(8,128)S(1)}, f32[8,66,1,128]{3,0,2,1:T(8,128)S(1)}, u32[]{:S(2)}, u32[]{:S(2)}) collective-permute-start(f32[8,66,1,128]{3,0,2,1:T(8,128)S(1)} %get-tuple-element.14), channel_id=1, source_target_pairs={{0,1},{1,2},{2,3},{3,4},{4,5},{5,6},{6,7},{8,9},{9,10},{10,11},{11... | collective-permute-start | bytes 811016 | tf_op jit(solution)/shard_map/ppermute | solution.py:15
  63.1 12.1 %copy-start.3 = (f32[8,64,16,128]{3,0,2,1:T(8,128)}, f32[8,64,16,128]{3,0,2,1:T(8,128)S(1)}, u32[]{:S(2)}) copy-start(f32[8,64,16,128]{3,0,2,1:T(8,128)S(1)} %get-tuple-element.7) | copy-start | bytes 12582916
  75.2 76.2 %collective-permute-start.12 = (f32[8,1,16,128]{3,0,2,1:T(8,128)}, f32[8,1,16,128]{3,0,2,1:T(8,128)S(1)}, u32[]{:S(2)}, u32[]{:S(2)}) collective-permute-start(f32[8,1,16,128]{3,0,2,1:T(8,128)} %get-tuple-element.16), channel_id=1, source_target_pairs={{8,0},{16,8},{24,16},{9,1},{17,9},{25,17},{10,2},{18,10},{26,18},{... | collective-permute-start | bytes 196616 | tf_op jit(solution)/shard_map/ppermute | solution.py:18
  76.5 74.8 %collective-permute-start.13 = (f32[8,1,16,128]{3,0,2,1:T(8,128)}, f32[8,1,16,128]{3,0,2,1:T(8,128)S(1)}, u32[]{:S(2)}, u32[]{:S(2)}) collective-permute-start(f32[8,1,16,128]{3,0,2,1:T(8,128)} %get-tuple-element.15), channel_id=1, source_target_pairs={{0,8},{8,16},{16,24},{1,9},{9,17},{17,25},{2,10},{10,18},{18,26},{... | collective-permute-start | bytes 196616 | tf_op jit(solution)/shard_map/ppermute | solution.py:15
  151.4 11.2 %copy-start.4 = (f32[8,64,16,128]{3,0,2,1:T(8,128)S(1)}, f32[8,64,16,128]{3,0,2,1:T(8,128)}, u32[]{:S(2)}) copy-start(f32[8,64,16,128]{3,0,2,1:T(8,128)} %copy-done.3) | copy-start | bytes 12582916
  151.4 11.2 %copy-start.13 = (f32[64,16,128]{2,1,0:T(8,128)S(1)}, f32[64,16,128]{2,1,0:T(8,128)}, u32[]{:S(2)}) copy-start(f32[64,16,128]{2,1,0:T(8,128)} %param.9) | copy-start | bytes 1572868
  152.6 8.5 %collective-permute-start.14 = (f32[8,66,1,128]{3,0,2,1:T(8,128)S(1)}, f32[8,66,1,128]{3,0,2,1:T(8,128)S(1)}, u32[]{:S(2)}, u32[]{:S(2)}) collective-permute-start(f32[8,66,1,128]{3,0,2,1:T(8,128)S(1)} %get-tuple-element.11), channel_id=1, source_target_pairs={{1,0},{2,1},{3,2},{4,3},{5,4},{6,5},{7,6},{9,8},{10,9},{11,10},{12... | collective-permute-start | bytes 811016 | tf_op jit(solution)/shard_map/ppermute | solution.py:18
  154.0 8.5 %collective-permute-start.15 = (f32[8,66,1,128]{3,0,2,1:T(8,128)S(1)}, f32[8,66,1,128]{3,0,2,1:T(8,128)S(1)}, u32[]{:S(2)}, u32[]{:S(2)}) collective-permute-start(f32[8,66,1,128]{3,0,2,1:T(8,128)S(1)} %get-tuple-element.12), channel_id=1, source_target_pairs={{0,1},{1,2},{2,3},{3,4},{4,5},{5,6},{6,7},{8,9},{9,10},{10,11},{11... | collective-permute-start | bytes 811016 | tf_op jit(solution)/shard_map/ppermute | solution.py:15
  158.9 13.5 %copy-start.1 = (f32[8,64,16,128]{3,0,2,1:T(8,128)S(1)}, f32[8,64,16,128]{3,0,2,1:T(8,128)}, u32[]{:S(2)}) copy-start(f32[8,64,16,128]{3,0,2,1:T(8,128)} %copy-done) | copy-start | bytes 12582916
  158.9 13.5 %copy-start.6 = (f32[8,64,16,128]{3,0,2,1:T(8,128)S(1)}, f32[8,64,16,128]{3,0,2,1:T(8,128)}, u32[]{:S(2)}) copy-start(f32[8,64,16,128]{3,0,2,1:T(8,128)} %get-tuple-element.8) | copy-start | bytes 12582916
  170.4 2.0 copy-start.7
  228.2 7.5 %copy-start.2 = (f32[8,64,16,128]{3,0,2,1:T(8,128)S(1)}, f32[8,64,16,128]{3,0,2,1:T(8,128)}, u32[]{:S(2)}) copy-start(f32[8,64,16,128]{3,0,2,1:T(8,128)} %copy-done) | copy-start | bytes 12582916
  228.2 7.5 %copy-start.5 = (f32[8,64,16,128]{3,0,2,1:T(8,128)S(1)}, f32[8,64,16,128]{3,0,2,1:T(8,128)}, u32[]{:S(2)}) copy-start(f32[8,64,16,128]{3,0,2,1:T(8,128)} %copy-done.3) | copy-start | bytes 12582916
